TPU v7x, 512 devices: a whole 4x8x8 slice. The times are simulated.
512 devices in a mesh: section: 8 (over x, core), expert: 64 (over z, y).
Axes of the slice: x: 4, y: 8, z: 8, core: 2. Of those that a mesh axis runs over, the one named last changes fastest.
Arguments:
- histories: bfloat16 [8, 8192, 5120], P('section', 'expert'), may hold values from -6 to 6
- page_map: int32 [8, 2, 2048], P('section', None, 'expert'), may hold values from 0 to 2047, as said below
- user_pages: int32 [8, 64, 4], P('section', 'expert'), may hold values from 1 to 16, 32 in all within a row
- tails: int32 [8, 64, 4], P('section', 'expert'), may hold values from 1 to 4
- routes: int32 [8, 8192, 2], P('section', 'expert'), may hold values from 0 to 31, all different within a row; in each aligned block of 128 rows (0 to 127, 128 to 255, ..., all dimensions but the last counted through in order) at most 16 rows name the same one
- out_proj: bfloat16 [8, 1024, 1024], P('section', 'expert'), may hold values from -0.1875 to 0.1875
- router: bfloat16 [8, 1024, 32], P('section'), may hold values from -0.75 to 0.75
- w_gate: bfloat16 [8, 1024, 32768], P('section', None, 'expert'), may hold values from -0.1875 to 0.1875
- w_up: bfloat16 [8, 1024, 32768], P('section', None, 'expert'), may hold values from -0.1875 to 0.1875
- w_down: bfloat16 [8, 32768, 1024], P('section', 'expert'), may hold values from -0.1875 to 0.1875
Outputs:
- handed: bfloat16 [8, 8192, 1024], P('section', 'expert')
Inputs may be any that keep to these rules, and one draw needn't show every extreme that they name: page_map[0] is a permutation of the pages of a section and page_map[1] its inverse; every device holds exactly 32 pages before and after; no device's pages send more than 1 pages to one device, and some send exactly 1. `user_pages`: the 4 entries of one device sum to 32, and the largest is 16. `routes`: A row names 2 different experts; among the rows of one device, no expert is named more than 16 times, a bound that some block reaches.
All inputs are finite; a program needn't handle non-finite values.
Results may differ from a plain program's by a relative error of at most 0.012.
Values may be sent and summed in bfloat16 or wider, within the bound.
No kernel may reach another device: no remote copies, remote signals or barrier semaphores. Data moves between devices by JAX's collectives and lax.ppermute only.
A program may use at most 64 MiB of HBM per device.

v0:
```python
import jax
import jax.numpy as jnp
from jax import lax
from jax.sharding import PartitionSpec as P

HEADS = 8


def swapped(shard, axis, apart):
    return lax.ppermute(shard, axis, [(i, i ^ 1 << apart) for i in range(lax.axis_size(axis))])


def from_behind(block, axis, distance):
    devices = range(lax.axis_size(axis))
    route = [((i - distance) % len(devices), i) for i in devices]
    return lax.ppermute(block, axis, route)


def layout_rows(counts, tail_rows, page_rows, row_count):
    starting = jnp.cumsum(counts) - counts
    length = (counts - 1) * page_rows + tail_rows
    row_index = jnp.arange(row_count, dtype=jnp.int32)
    page_of = row_index // page_rows
    owner_of = jnp.sum((starting[None, :] <= page_of[:, None]).astype(jnp.int32), axis=1) - 1
    member = owner_of[:, None] == jnp.arange(counts.shape[0], dtype=jnp.int32)[None, :]
    offset = jnp.sum(jnp.where(member, starting[None, :] * page_rows, 0), axis=1)
    spread = jnp.sum(jnp.where(member, length[None, :], 0), axis=1)
    return (owner_of, row_index - offset, spread)


def attend(balanced, counts, tail_rows, page_rows):
    row_count = balanced.shape[0]
    model_width = balanced.shape[1] // 5
    head_dim = model_width // HEADS
    owner_of, position, spread = layout_rows(counts, tail_rows, page_rows, row_count)
    allowed = (
        (owner_of[:, None] == owner_of[None, :])
        & (position[None, :] <= position[:, None])
        & (position[None, :] < spread[None, :])
    )
    queries = balanced[:, :model_width].reshape(row_count, HEADS, head_dim)
    key_rows = balanced[:, model_width : 2 * model_width].reshape(row_count, HEADS, head_dim)
    values = balanced[:, 2 * model_width : 3 * model_width].reshape(row_count, HEADS, head_dim)
    scores = jnp.einsum(
        "qhd,khd->hqk", queries, key_rows, preferred_element_type=jnp.float32
    ) * head_dim ** (-0.5)
    weights = (
        jnp.where(allowed[None], jax.nn.silu(scores), 0.0)
        / spread.astype(jnp.float32)[None, :, None]
    )
    weights = weights.astype(jnp.bfloat16)
    attended = jnp.einsum(
        "hqk,khd->qhd", weights, values, preferred_element_type=jnp.float32
    ).reshape(row_count, model_width)
    average = jnp.mean(attended, axis=1, keepdims=True)
    centered = attended - average
    variance = jnp.mean(centered * centered, axis=1, keepdims=True)
    gating = balanced[:, 3 * model_width : 4 * model_width].astype(jnp.float32)
    return (centered * lax.rsqrt(variance + 1e-05) * gating).astype(jnp.bfloat16)


def gate_share(normed, router, routes):
    logits = jnp.dot(normed, router, preferred_element_type=jnp.float32)
    scores = jax.nn.sigmoid(logits)
    picked = routes[:, :, None] == jnp.arange(router.shape[1], dtype=jnp.int32)[None, None, :]
    chosen = jnp.sum(jnp.where(picked, scores[:, None, :], 0.0), axis=2)
    return chosen / jnp.sum(chosen, axis=1, keepdims=True)


def slot_table(routes, experts, capacity):
    pair_count = routes.shape[0] * routes.shape[1]
    chosen = routes.reshape(-1)
    onehot = (chosen[:, None] == jnp.arange(experts, dtype=jnp.int32)[None, :]).astype(jnp.int32)
    before = jnp.cumsum(onehot, axis=0) - onehot
    ranking = jnp.sum(before * onehot, axis=1)
    slot_of_pair = chosen * capacity + ranking
    matches = slot_of_pair[None, :] == jnp.arange(experts * capacity, dtype=jnp.int32)[:, None]
    source_token = (
        jnp.sum(jnp.where(matches, jnp.arange(pair_count, dtype=jnp.int32)[None, :], 0), axis=1)
        // 2
    )
    return (slot_of_pair, source_token)


def whole_expert(incoming, gate_full, up_full, down_full):
    flat_rows = incoming.reshape(-1, incoming.shape[-1])
    gate_act = jnp.dot(flat_rows, gate_full, preferred_element_type=jnp.float32)
    up_act = jnp.dot(flat_rows, up_full, preferred_element_type=jnp.float32)
    hidden = (jax.nn.silu(gate_act) * up_act).astype(jnp.bfloat16)
    half_units = gate_full.shape[1] // 2
    first_part = jnp.dot(
        hidden[:, :half_units], down_full[:half_units], preferred_element_type=jnp.float32
    ).astype(jnp.bfloat16)
    second_part = jnp.dot(
        hidden[:, half_units:], down_full[half_units:], preferred_element_type=jnp.float32
    ).astype(jnp.bfloat16)
    summed = (first_part.astype(jnp.float32) + second_part.astype(jnp.float32)).astype(jnp.bfloat16)
    return summed.reshape(incoming.shape)


def shards(histories, page_map, user_pages, tails, routes, out_proj, router, w_gate, w_up, w_down):
    devices = lax.axis_size("expert")
    parity = lax.axis_index("expert") % 2
    row_count = histories.shape[1]
    stacked_width = histories.shape[2]
    model_width = stacked_width // 5
    pages_dev = page_map.shape[2]
    page_rows = row_count // pages_dev
    page_slots = (pages_dev + devices - 1) // devices
    page_block = histories[0].reshape(pages_dev, page_rows, stacked_width)
    target = page_map[0, 0]
    target_dev = target // pages_dev
    earlier = (target_dev[None, :] == target_dev[:, None]) & (target[None, :] < target[:, None])
    position = target_dev * page_slots + jnp.sum(earlier.astype(jnp.int32), axis=1)
    matches = position[None, :] == jnp.arange(devices * page_slots, dtype=jnp.int32)[:, None]
    chosen_page = jnp.sum(
        jnp.where(matches, jnp.arange(pages_dev, dtype=jnp.int32)[None, :], 0), axis=1
    )
    outgoing = page_block[chosen_page]
    arrived = lax.all_to_all(outgoing, "expert", split_axis=0, concat_axis=0, tiled=True)
    anchor = page_map[0, 1]
    anchor_dev = anchor // pages_dev
    ordering = jnp.arange(pages_dev, dtype=jnp.int32)
    sooner = (anchor_dev[None, :] == anchor_dev[:, None]) & (ordering[None, :] < ordering[:, None])
    where_from = anchor_dev * page_slots + jnp.sum(sooner.astype(jnp.int32), axis=1)
    balanced = arrived[where_from].reshape(row_count, stacked_width)
    mixed_in = attend(balanced, user_pages[0, 0], tails[0, 0], page_rows)
    projected = jnp.dot(
        mixed_in,
        lax.all_gather(out_proj, "expert", axis=1, tiled=True)[0],
        preferred_element_type=jnp.float32,
    )
    resid = (balanced[:, 4 * model_width :].astype(jnp.float32) + projected).astype(jnp.bfloat16)
    resid_wide = resid.astype(jnp.float32)
    normed = (
        resid_wide * lax.rsqrt(jnp.mean(resid_wide * resid_wide, axis=1, keepdims=True) + 1e-06)
    ).astype(jnp.bfloat16)
    experts = router.shape[2]
    capacity = 4 * row_count // experts
    share = gate_share(normed, router[0], routes[0])
    slot_of_pair, source_token = slot_table(routes[0], experts, capacity)
    packed = normed[source_token].reshape(experts, capacity, model_width)
    is_odd = parity == 1
    half_units = w_gate.shape[2]
    gate_up = jnp.concatenate([w_gate[0], w_up[0]], axis=1)
    other_gate_up = swapped(gate_up, "expert", 0)
    other_down = swapped(w_down[0], "expert", 0)
    own_gate = gate_up[:, :half_units]
    own_up = gate_up[:, half_units:]
    other_gate = other_gate_up[:, :half_units]
    other_up = other_gate_up[:, half_units:]
    gate_full = jnp.where(
        is_odd,
        jnp.concatenate([other_gate, own_gate], axis=1),
        jnp.concatenate([own_gate, other_gate], axis=1),
    )
    up_full = jnp.where(
        is_odd,
        jnp.concatenate([other_up, own_up], axis=1),
        jnp.concatenate([own_up, other_up], axis=1),
    )
    down_full = jnp.where(
        is_odd,
        jnp.concatenate([other_down, w_down[0]], axis=0),
        jnp.concatenate([w_down[0], other_down], axis=0),
    )
    half_cap = capacity // 2
    sent_rows = packed.reshape(experts * 2, half_cap, model_width)
    own_rows = lax.all_to_all(sent_rows, "expert", split_axis=0, concat_axis=0, tiled=True)
    served = whole_expert(own_rows, gate_full, up_full, down_full)
    came_back = lax.all_to_all(served, "expert", split_axis=0, concat_axis=0, tiled=True)
    result = came_back.reshape(experts, capacity, model_width)
    picked = result.reshape(experts * capacity, model_width)[slot_of_pair]
    picked = picked.reshape(row_count, 2, model_width).astype(jnp.float32)
    mixture = jnp.sum(picked * share[:, :, None], axis=1)
    output_rows = (resid_wide + mixture).astype(jnp.bfloat16)
    return from_behind(output_rows[None], "section", 1)


def solution(mesh):
    in_specs = (
        P("section", "expert", None),
        P("section", None, "expert"),
        P("section", "expert", None),
        P("section", "expert", None),
        P("section", "expert", None),
        P("section", "expert", None),
        P("section", None, None),
        P("section", None, "expert"),
        P("section", None, "expert"),
        P("section", "expert", None),
    )
    out_specs = P("section", "expert", None)
    return jax.shard_map(shards, mesh=mesh, in_specs=in_specs, out_specs=out_specs, check_vma=False)
```

profile of v0, /device:TPU:8, one launch (start us, length us, event | category | flops | bytes accessed | tf_op | source)
XLA Modules:
  0.0 289.1 jit_solution(12892616485323434839)
XLA Ops:
  8.3 2.6 reshape_squeeze.6
  10.9 4.2 %gather_fusion = bf16[64,4,5120]{2,1,0:T(4,128)(2,1)} fusion(bf16[32,4,5120]{2,1,0:T(4,128)(2,1)S(1)} %reshape_squeeze.6, s32[1024]{0:T(1024)S(1)} %pad_clamp_fusion.3), kind=kCustom, calls=%fused_computation | custom fusion | bytes 5243136 | tf_op jit(solution)/shard_map/gather | solution.py:119
  15.1 16.6 %all-to-all-start = ((bf16[64,4,5120]{2,1,0:T(4,128)(2,1)}), bf16[64,4,5120]{2,1,0:T(4,128)(2,1)S(1)}, u32[]{:S(2)}, u32[]{:S(2)}) async-start(bf16[64,4,5120]{2,1,0:T(4,128)(2,1)} %gather_fusion), calls=%async_computation | async-start | bytes 5242880 | tf_op jit(solution)/shard_map/all_to_all | solution.py:120
  32.5 3.1 %pad_maximum_fusion.1 = bf16[1024,1024]{1,0:T(8,128)(2,1)} fusion(bf16[1024,512]{1,0:T(8,128)(2,1)} %bitcast.121, bf16[1024,512]{1,0:T(8,128)(2,1)} %bitcast.119), kind=kLoop, calls=%fused_computation.5 | loop fusion | flops 4194304 | bytes 4194304 | tf_op jit(solution)/shard_map/concatenate | solution.py:145
  35.6 2.4 collective-permute-start
  40.0 57.6 %all-to-all-done = bf16[64,4,5120]{2,1,0:T(4,128)(2,1)S(1)} async-done(((bf16[64,4,5120]{2,1,0:T(4,128)(2,1)}), bf16[64,4,5120]{2,1,0:T(4,128)(2,1)S(1)}, u32[]{:S(2)}, u32[]{:S(2)}) %all-to-all-start) | async-done | bytes 2621472 | tf_op jit(solution)/shard_map/all_to_all | solution.py:120
  97.6 2.7 gather_fusion.1
  100.3 2.5 reshape.543
  104.4 52.7 %all-gather.2.cloned.1.call-done = bf16[1,1024,1024]{2,1,0:T(8,128)(2,1)} async-done(((bf16[1,16,1024]{2,1,0:T(8,128)(2,1)}), bf16[1,1024,1024]{2,1,0:T(8,128)(2,1)}) %all-gather.2.cloned.1.call-update) | async-done | bytes 2097168 | tf_op jit(solution)/shard_map/all_gather | solution.py:130
  157.1 2.2 multiply_reduce_fusion.1
  159.4 2.8 gather_fusion.2
  162.2 10.1 %all-to-all-start.1 = ((bf16[64,8,1024]{2,1,0:T(8,128)(2,1)}), bf16[64,8,1024]{2,1,0:T(8,128)(2,1)}, u32[]{:S(2)}, u32[]{:S(2)}) async-start(bf16[64,8,1024]{2,1,0:T(8,128)(2,1)} %bitcast.20), calls=%async_computation.1 | async-start | bytes 2097152 | tf_op jit(solution)/shard_map/all_to_all | solution.py:169
  172.2 2.6 collective-permute-start.1
  174.9 39.3 %collective-permute-done.1 = bf16[512,1024]{1,0:T(8,128)(2,1)} collective-permute-done((bf16[512,1024]{1,0:T(8,128)(2,1)S(1)}, bf16[512,1024]{1,0:T(8,128)(2,1)}, u32[]{:S(2)}, u32[]{:S(2)}) %collective-permute-start.1) | collective-permute-done | bytes 1048608 | tf_op jit(solution)/shard_map/ppermute | solution.py:10
  214.2 4.1 %maximum_select_fusion = bf16[1024,1024]{1,0:T(8,128)(2,1)} fusion(bf16[512,1024]{1,0:T(8,128)(2,1)S(1)} %bitcast.118, bf16[512,1024]{1,0:T(8,128)(2,1)} %collective-permute-done.1, pred[]{:T(512)S(6)} %eq.150), kind=kLoop, calls=%fused_computation.19 | loop fusion | flops 9437184 | bytes 4194305 | tf_op jit(solution)/shard_map/jit(_where)/select_n | solution.py:162
  218.3 3.1 %fusion.68 = (bf16[1024,512]{1,0:T(8,128)(2,1)}, bf16[1024,512]{1,0:T(8,128)(2,1)}) fusion(bf16[1024,1024]{1,0:T(8,128)(2,1)} %collective-permute-done), kind=kLoop, calls=%fused_computation.141 | loop fusion | bytes 4194304 | tf_op jit(solution)/shard_map/slice | solution.py:151
  221.3 3.3 %fusion.1 = f32[512,1024]{1,0:T(8,128)S(1)} fusion(bf16[1024,512]{1,0:T(8,128)(2,1)S(1)} %bitcast.120, bf16[1024,512]{1,0:T(8,128)(2,1)} %get-tuple-element.12, pred[]{:T(512)S(6)} %eq.150, bf16[64,8,1024]{2,1,0:T(8,128)(2,1)} %all-to-all-done.1), kind=kOutput, calls=%fused_computation.8 | convolution fusion | flops 1083179008 | bytes 5242881 | tf_op jit(solution)/shard_map/dot_general | solution.py:87
  224.7 3.8 %multiply_convert_fusion = bf16[512,1024]{1,0:T(8,128)(2,1)S(1)} fusion(f32[512,1024]{1,0:T(8,128)S(1)} %fusion.1, bf16[1024,512]{1,0:T(8,128)(2,1)S(1)} %bitcast.122, bf16[1024,512]{1,0:T(8,128)(2,1)S(1)} %copy-done.5, pred[]{:T(512)S(6)} %eq.150, bf16[64,8,1024]{2,1,0:T(8,128)(2,1)} %all-to-all-done.1), kind=kOutput, calls=%fused_computation.23 | convolution fusion | flops 1086324736 | bytes 6291457 | tf_op jit(solution)/shard_map/dot_general | solution.py:88
  229.2 1.7 fusion.18
  230.9 12.6 %all-to-all-start.2 = ((bf16[64,8,1024]{2,1,0:T(8,128)(2,1)}), bf16[64,8,1024]{2,1,0:T(8,128)(2,1)S(1)}, u32[]{:S(2)}, u32[]{:S(2)}) async-start(bf16[64,8,1024]{2,1,0:T(8,128)(2,1)} %fusion.18), calls=%async_computation.2 | async-start | bytes 2097152 | tf_op jit(solution)/shard_map/all_to_all | solution.py:171
  244.2 27.0 %all-to-all-done.2 = bf16[64,8,1024]{2,1,0:T(8,128)(2,1)S(1)} async-done(((bf16[64,8,1024]{2,1,0:T(8,128)(2,1)}), bf16[64,8,1024]{2,1,0:T(8,128)(2,1)S(1)}, u32[]{:S(2)}, u32[]{:S(2)}) %all-to-all-start.2) | async-done | bytes 1048608 | tf_op jit(solution)/shard_map/all_to_all | solution.py:171
  271.3 1.2 gather_fusion.3
  273.1 1.3 multiply_reduce_fusion
  274.5 7.0 %collective-permute-done.2 = bf16[1,128,1024]{2,1,0:T(8,128)(2,1)S(1)} collective-permute-done((bf16[1,128,1024]{2,1,0:T(8,128)(2,1)S(1)}, bf16[1,128,1024]{2,1,0:T(8,128)(2,1)S(1)}, u32[]{:S(2)}, u32[]{:S(2)}) %collective-permute-start.2) | collective-permute-done | bytes 262176 | tf_op jit(solution)/shard_map/ppermute | solution.py:16
  (81 shorter events, 9.0 us)
Async XLA Ops:
  6.5 237.3 %copy-start = (bf16[1,1024,32]{1,2,0:T(8,128)(2,1)S(1)}, bf16[1,1024,32]{1,2,0:T(8,128)(2,1)}, u32[]{:S(2)}) copy-start(bf16[1,1024,32]{1,2,0:T(8,128)(2,1)} %param.16) | copy-start | bytes 196612
  15.1 82.5 %all-to-all-start = ((bf16[64,4,5120]{2,1,0:T(4,128)(2,1)}), bf16[64,4,5120]{2,1,0:T(4,128)(2,1)S(1)}, u32[]{:S(2)}, u32[]{:S(2)}) async-start(bf16[64,4,5120]{2,1,0:T(4,128)(2,1)} %gather_fusion), calls=%async_computation | async-start | bytes 5242880 | tf_op jit(solution)/shard_map/all_to_all | solution.py:120
  31.7 125.4 %all-gather.2.cloned.1.call-start = ((), (), s32[]{:S(2)}) async-start(), calls=%async_computation.3 | async-start | bytes 2129920 | tf_op jit(solution)/shard_map/all_gather | solution.py:130
  32.4 5.5 %copy-start.6 = (s32[1,128,2]{1,2,0:T(2,128)S(1)}, s32[1,128,2]{1,2,0:T(2,128)}, u32[]{:S(2)}) copy-start(s32[1,128,2]{1,2,0:T(2,128)} %param.14) | copy-start | bytes 3076
  32.4 5.9 %copy-start.8 = (s32[1,1,4]{2,1,0:T(1,128)S(1)}, s32[1,1,4]{2,1,0:T(1,128)}, u32[]{:S(2)}) copy-start(s32[1,1,4]{2,1,0:T(1,128)} %param.12) | copy-start | bytes 52
  32.4 6.1 %copy-start.9 = (s32[1,1,4]{2,1,0:T(1,128)S(1)}, s32[1,1,4]{2,1,0:T(1,128)}, u32[]{:S(2)}) copy-start(s32[1,1,4]{2,1,0:T(1,128)} %param.13) | copy-start | bytes 52
  32.5 7.1 %copy-start.7 = (s32[1,2,32]{2,1,0:T(2,128)S(1)}, s32[1,2,32]{2,1,0:T(2,128)}, u32[]{:S(2)}) copy-start(s32[1,2,32]{2,1,0:T(2,128)} %param.11) | copy-start | bytes 772
  35.6 182.7 %collective-permute-start = (bf16[1024,1024]{1,0:T(8,128)(2,1)}, bf16[1024,1024]{1,0:T(8,128)(2,1)}, u32[]{:S(2)}, u32[]{:S(2)}) collective-permute-start(bf16[1024,1024]{1,0:T(8,128)(2,1)} %pad_maximum_fusion.1), channel_id=1, source_target_pairs={{0,1},{1,0},{2,3},{3,2},{4,5},{5,4},{6,7},{7,6},{8,9},{9,8},{10,11... | collective-permute-start | bytes 6291464 | tf_op jit(solution)/shard_map/ppermute | solution.py:10
  162.2 10.1 %copy-start.2 = (bf16[1,512,1024]{2,1,0:T(8,128)(2,1)S(1)}, bf16[1,512,1024]{2,1,0:T(8,128)(2,1)}, u32[]{:S(2)}) copy-start(bf16[1,512,1024]{2,1,0:T(8,128)(2,1)} %param.19) | copy-start | bytes 3145732
  162.2 59.2 %all-to-all-start.1 = ((bf16[64,8,1024]{2,1,0:T(8,128)(2,1)}), bf16[64,8,1024]{2,1,0:T(8,128)(2,1)}, u32[]{:S(2)}, u32[]{:S(2)}) async-start(bf16[64,8,1024]{2,1,0:T(8,128)(2,1)} %bitcast.20), calls=%async_computation.1 | async-start | bytes 2097152 | tf_op jit(solution)/shard_map/all_to_all | solution.py:169
  172.2 41.9 %collective-permute-start.1 = (bf16[512,1024]{1,0:T(8,128)(2,1)S(1)}, bf16[512,1024]{1,0:T(8,128)(2,1)}, u32[]{:S(2)}, u32[]{:S(2)}) collective-permute-start(bf16[512,1024]{1,0:T(8,128)(2,1)S(1)} %bitcast.117), channel_id=1, source_target_pairs={{0,1},{1,0},{2,3},{3,2},{4,5},{5,4},{6,7},{7,6},{8,9},{9,8},{10,11... | collective-permute-start | bytes 3145736 | tf_op jit(solution)/shard_map/ppermute | solution.py:10
  218.3 3.1 %copy-start.3 = (bf16[1,1024,512]{2,1,0:T(8,128)(2,1)S(1)}, bf16[1,1024,512]{2,1,0:T(8,128)(2,1)}, u32[]{:S(2)}) copy-start(bf16[1,1024,512]{2,1,0:T(8,128)(2,1)} %param.17) | copy-start | bytes 3145732
  221.3 3.3 %copy-start.4 = (bf16[1,1024,512]{2,1,0:T(8,128)(2,1)S(1)}, bf16[1,1024,512]{2,1,0:T(8,128)(2,1)}, u32[]{:S(2)}) copy-start(bf16[1,1024,512]{2,1,0:T(8,128)(2,1)} %param.18) | copy-start | bytes 3145732
  221.3 3.3 %copy-start.5 = (bf16[1024,512]{1,0:T(8,128)(2,1)S(1)}, bf16[1024,512]{1,0:T(8,128)(2,1)}, u32[]{:S(2)}) copy-start(bf16[1024,512]{1,0:T(8,128)(2,1)} %get-tuple-element.11) | copy-start | bytes 3145732
  224.7 3.8 %copy-start.1 = (bf16[1024,1024]{1,0:T(8,128)(2,1)S(1)}, bf16[1024,1024]{1,0:T(8,128)(2,1)}, u32[]{:S(2)}) copy-start(bf16[1024,1024]{1,0:T(8,128)(2,1)} %maximum_select_fusion) | copy-start | bytes 6291460
  230.9 40.4 %all-to-all-start.2 = ((bf16[64,8,1024]{2,1,0:T(8,128)(2,1)}), bf16[64,8,1024]{2,1,0:T(8,128)(2,1)S(1)}, u32[]{:S(2)}, u32[]{:S(2)}) async-start(bf16[64,8,1024]{2,1,0:T(8,128)(2,1)} %fusion.18), calls=%async_computation.2 | async-start | bytes 2097152 | tf_op jit(solution)/shard_map/all_to_all | solution.py:171
  274.5 7.0 %collective-permute-start.2 = (bf16[1,128,1024]{2,1,0:T(8,128)(2,1)S(1)}, bf16[1,128,1024]{2,1,0:T(8,128)(2,1)S(1)}, u32[]{:S(2)}, u32[]{:S(2)}) collective-permute-start(bf16[1,128,1024]{2,1,0:T(8,128)(2,1)S(1)} %fusion.44), channel_id=1, source_target_pairs={{448,0},{0,64},{64,128},{128,192},{192,256},{256,320},{320,384},{3... | collective-permute-start | bytes 786440 | tf_op jit(solution)/shard_map/ppermute | solution.py:16
Sparse Core Ops, SparseCore 0:
  35.6 121.4 all-gather.1
where the time goes:
time: 290 us; the launch traced here: 289 us
  waiting for transfers between devices  184 us (63%)
  starting transfers between devices  44.3 us (15%)
  local copies, waits for them, and re-layouts  22.7 us (8%)
  between operations  13.8 us (5%)
  matrix products  12.5 us (4%)
  other arithmetic  11.4 us (4%)
    all_to_all x1, waiting for transfers between devices, shards(): lax.all_to_all(outgoing, 'expert', split_axis=0, concat_axis=0, tiled=True)  57.6 us
    all_gather x1, waiting for transfers between devices, shards(): lax.all_gather(out_proj, 'expert', axis=1, tiled=True)[0]  52.7 us
    ppermute x2, waiting for transfers between devices, swapped(): lax.ppermute(shard, axis, [(i, i ^ 1 << apart) for i in range(lax.axis_si...  39.3 us
    all_to_all x1, waiting for transfers between devices, shards(): lax.all_to_all(served, 'expert', split_axis=0, concat_axis=0, tiled=True)  27 us
    all_to_all x1, starting transfers between devices, shards(): lax.all_to_all(outgoing, 'expert', split_axis=0, concat_axis=0, tiled=True)  16.6 us
    all_to_all x1, starting transfers between devices, shards(): lax.all_to_all(served, 'expert', split_axis=0, concat_axis=0, tiled=True)  12.6 us
    all_to_all x1, starting transfers between devices, shards(): lax.all_to_all(sent_rows, 'expert', split_axis=0, concat_axis=0, tiled=True)  10.1 us
    ppermute x1, waiting for transfers between devices, from_behind(): return lax.ppermute(block, axis, route)  6.99 us
  transfers between devices with their start and end apart: 7, of which 5 were waited for; matrix products, arithmetic and copies ran while one was open for 9% of the time, Pallas kernels for 0%

commit v1 on v0

--- a/solution.py
+++ b/solution.py
@@ -127,7 +127,9 @@
     mixed_in = attend(balanced, user_pages[0, 0], tails[0, 0], page_rows)
     projected = jnp.dot(
         mixed_in,
-        lax.all_gather(out_proj, "expert", axis=1, tiled=True)[0],
+        jnp.concatenate(
+            lax.all_to_all(jnp.stack([out_proj] * lax.axis_size("expert")), "expert", 0, 0), axis=1
+        )[0],
         preferred_element_type=jnp.float32,
     )
     resid = (balanced[:, 4 * model_width :].astype(jnp.float32) + projected).astype(jnp.bfloat16)

time: 290 us -> 304 us (1.048)
  blocking collectives: 0 us -> 81.2 us
  waiting for transfers between devices: 184 us -> 138 us
  between operations: 13.8 us -> 0.43 us
  starting transfers between devices: 44.3 us -> 35.4 us
    all_to_all x0 -> x1, blocking collectives: none -> 81.2 us  [shards(): lax.all_to_all(outgoing, 'expert', split_axis=0, concat_axis=0, tiled=True)]
    all_gather x1 -> x0, waiting for transfers between devices: 52.7 us -> none  [shards(): lax.all_gather(out_proj, 'expert', axis=1, tiled=True)[0]]
    ppermute x2, waiting for transfers between devices: 39.3 us -> 66.9 us  [swapped(): lax.ppermute(shard, axis, [(i, i ^ 1 << apart) for i in range(lax.axis_si...]
    all_to_all x1, waiting for transfers between devices: 57.6 us -> 36.7 us  [shards(): lax.all_to_all(jnp.stack([out_proj] * lax.axis_size('expert')), 'expert',...]
    all_to_all x1, starting transfers between devices: 16.6 us -> 9.84 us  [shards(): lax.all_to_all(jnp.stack([out_proj] * lax.axis_size('expert')), 'expert',...]
  transfers between devices with their start and end apart: 7 -> 6, of which waited for: 5 -> 4; matrix products, arithmetic and copies ran while one was open for 9% -> 8% of each run, Pallas kernels for 0% -> 0%
where the time goes in v1:
time: 304 us; the launch traced here: 303 us
  waiting for transfers between devices  138 us (45%)
  blocking collectives  81.2 us (27%)
  starting transfers between devices  35.4 us (12%)
  local copies, waits for them, and re-layouts  25 us (8%)
  matrix products  11.9 us (4%)
  other arithmetic  11.1 us (4%)
    all_to_all x1, blocking collectives, shards(): lax.all_to_all(outgoing, 'expert', split_axis=0, concat_axis=0, tiled=True)  81.2 us
    ppermute x2, waiting for transfers between devices, swapped(): lax.ppermute(shard, axis, [(i, i ^ 1 << apart) for i in range(lax.axis_si...  66.9 us
    all_to_all x1, waiting for transfers between devices, shards(): lax.all_to_all(jnp.stack([out_proj] * lax.axis_size('expert')), 'expert',...  36.7 us
    all_to_all x1, waiting for transfers between devices, shards(): lax.all_to_all(served, 'expert', split_axis=0, concat_axis=0, tiled=True)  27.5 us
    all_to_all x1, starting transfers between devices, shards(): lax.all_to_all(served, 'expert', split_axis=0, concat_axis=0, tiled=True)  12.7 us
    all_to_all x1, starting transfers between devices, shards(): lax.all_to_all(jnp.stack([out_proj] * lax.axis_size('expert')), 'expert',...  9.84 us
    all_to_all x1, starting transfers between devices, shards(): lax.all_to_all(sent_rows, 'expert', split_axis=0, concat_axis=0, tiled=True)  7.91 us
    ppermute x1, waiting for transfers between devices, from_behind(): return lax.ppermute(block, axis, route)  6.99 us
  transfers between devices with their start and end apart: 6, of which 4 were waited for; matrix products, arithmetic and copies ran while one was open for 8% of the time, Pallas kernels for 0%

profile of v1, /device:TPU:8, one launch (start us, length us, event | category | flops | bytes accessed | tf_op | source)
XLA Modules:
  0.0 303.2 jit_solution(114096800394732750)
XLA Ops:
  1.8 2.6 reshape_squeeze.6
  4.3 4.2 %gather_fusion = bf16[64,4,5120]{2,1,0:T(4,128)(2,1)} fusion(bf16[32,4,5120]{2,1,0:T(4,128)(2,1)S(1)} %reshape_squeeze.6, s32[1024]{0:T(1024)S(1)} %pad_clamp_fusion.3), kind=kCustom, calls=%fused_computation | custom fusion | bytes 5243136 | tf_op jit(solution)/shard_map/gather | solution.py:119
  8.5 81.2 %all_to_all.20 = bf16[64,4,5120]{2,1,0:T(4,128)(2,1)} all-to-all(bf16[64,4,5120]{2,1,0:T(4,128)(2,1)} %gather_fusion), channel_id=1, replica_groups=mesh['section'=8,'expert'=64] {'expert'}, dimensions={0} | all-to-all | bytes 5242880 | tf_op jit(solution)/shard_map/all_to_all | solution.py:120
  89.7 1.7 stack.2
  91.4 9.8 %all-to-all-start.1 = ((bf16[64,1,16,1024]{3,2,1,0:T(8,128)(2,1)}), bf16[64,1,16,1024]{3,2,1,0:T(8,128)(2,1)S(1)}, u32[]{:S(2)}, u32[]{:S(2)}) async-start(bf16[64,1,16,1024]{3,2,1,0:T(8,128)(2,1)} %stack.2), calls=%async_computation.1 | async-start | bytes 4194304 | tf_op jit(solution)/shard_map/all_to_all | solution.py:131
  101.3 2.8 pad_maximum_fusion.1
  104.1 2.4 collective-permute-start
  108.5 3.4 %gather_fusion.1 = bf16[32,4,5120]{2,1,0:T(4,128)(2,1)S(1)} fusion(bf16[64,4,5120]{2,1,0:T(4,128)(2,1)} %all_to_all.20, s32[1024]{0:T(1024)S(1)} %pad_clamp_fusion.2), kind=kCustom, calls=%fused_computation.1 | custom fusion | bytes 2621568 | tf_op jit(solution)/shard_map/gather | solution.py:126
  112.0 1.2 reshape.546
  115.9 36.7 %all-to-all-done.1 = bf16[64,1,16,1024]{3,2,1,0:T(8,128)(2,1)S(1)} async-done(((bf16[64,1,16,1024]{3,2,1,0:T(8,128)(2,1)}), bf16[64,1,16,1024]{3,2,1,0:T(8,128)(2,1)S(1)}, u32[]{:S(2)}, u32[]{:S(2)}) %all-to-all-start.1) | async-done | bytes 2097184 | tf_op jit(solution)/shard_map/all_to_all | solution.py:131
  152.6 1.6 multiply_reduce_fusion.1
  154.3 2.8 gather_fusion.2
  157.1 7.9 %all-to-all-start.2 = ((bf16[64,8,1024]{2,1,0:T(8,128)(2,1)}), bf16[64,8,1024]{2,1,0:T(8,128)(2,1)}, u32[]{:S(2)}, u32[]{:S(2)}) async-start(bf16[64,8,1024]{2,1,0:T(8,128)(2,1)} %bitcast.21), calls=%async_computation.2 | async-start | bytes 2097152 | tf_op jit(solution)/shard_map/all_to_all | solution.py:171
  165.0 2.6 collective-permute-start.1
  167.7 66.9 %collective-permute-done.1 = bf16[512,1024]{1,0:T(8,128)(2,1)} collective-permute-done((bf16[512,1024]{1,0:T(8,128)(2,1)S(1)}, bf16[512,1024]{1,0:T(8,128)(2,1)}, u32[]{:S(2)}, u32[]{:S(2)}) %collective-permute-start.1) | collective-permute-done | bytes 1048608 | tf_op jit(solution)/shard_map/ppermute | solution.py:10
  234.6 4.1 %maximum_select_fusion = bf16[1024,1024]{1,0:T(8,128)(2,1)} fusion(bf16[512,1024]{1,0:T(8,128)(2,1)S(1)} %bitcast.111, bf16[512,1024]{1,0:T(8,128)(2,1)} %collective-permute-done.1, pred[]{:T(512)S(6)} %eq.150), kind=kLoop, calls=%fused_computation.19 | loop fusion | flops 9437184 | bytes 4194305 | tf_op jit(solution)/shard_map/jit(_where)/select_n | solution.py:164
  238.7 3.1 %fusion.59 = (bf16[1024,512]{1,0:T(8,128)(2,1)}, bf16[1024,512]{1,0:T(8,128)(2,1)}) fusion(bf16[1024,1024]{1,0:T(8,128)(2,1)} %collective-permute-done), kind=kLoop, calls=%fused_computation.139 | loop fusion | bytes 4194304 | tf_op jit(solution)/shard_map/slice | solution.py:153
  241.8 3.3 %fusion.1 = f32[512,1024]{1,0:T(8,128)S(1)} fusion(bf16[1024,512]{1,0:T(8,128)(2,1)S(1)} %bitcast.113, bf16[1024,512]{1,0:T(8,128)(2,1)} %get-tuple-element.12, pred[]{:T(512)S(6)} %eq.150, bf16[64,8,1024]{2,1,0:T(8,128)(2,1)} %all-to-all-done.2), kind=kOutput, calls=%fused_computation.8 | convolution fusion | flops 1083179008 | bytes 5242881 | tf_op jit(solution)/shard_map/dot_general | solution.py:87
  245.1 3.8 %multiply_convert_fusion = bf16[512,1024]{1,0:T(8,128)(2,1)S(1)} fusion(f32[512,1024]{1,0:T(8,128)S(1)} %fusion.1, bf16[1024,512]{1,0:T(8,128)(2,1)S(1)} %bitcast.115, bf16[1024,512]{1,0:T(8,128)(2,1)S(1)} %copy-done.6, pred[]{:T(512)S(6)} %eq.150, bf16[64,8,1024]{2,1,0:T(8,128)(2,1)} %all-to-all-done.2), kind=kOutput, calls=%fused_computation.21 | convolution fusion | flops 1086324736 | bytes 6291457 | tf_op jit(solution)/shard_map/dot_general | solution.py:88
  249.6 1.7 fusion.16
  251.3 12.7 %all-to-all-start.3 = ((bf16[64,8,1024]{2,1,0:T(8,128)(2,1)}), bf16[64,8,1024]{2,1,0:T(8,128)(2,1)S(1)}, u32[]{:S(2)}, u32[]{:S(2)}) async-start(bf16[64,8,1024]{2,1,0:T(8,128)(2,1)} %fusion.16), calls=%async_computation.3 | async-start | bytes 2097152 | tf_op jit(solution)/shard_map/all_to_all | solution.py:173
  264.7 27.5 %all-to-all-done.3 = bf16[64,8,1024]{2,1,0:T(8,128)(2,1)S(1)} async-done(((bf16[64,8,1024]{2,1,0:T(8,128)(2,1)}), bf16[64,8,1024]{2,1,0:T(8,128)(2,1)S(1)}, u32[]{:S(2)}, u32[]{:S(2)}) %all-to-all-start.3) | async-done | bytes 1048608 | tf_op jit(solution)/shard_map/all_to_all | solution.py:173
  294.0 1.3 multiply_reduce_fusion
  295.5 7.0 %collective-permute-done.2 = bf16[1,128,1024]{2,1,0:T(8,128)(2,1)S(1)} collective-permute-done((bf16[1,128,1024]{2,1,0:T(8,128)(2,1)S(1)}, bf16[1,128,1024]{2,1,0:T(8,128)(2,1)S(1)}, u32[]{:S(2)}, u32[]{:S(2)}) %collective-permute-start.2) | collective-permute-done | bytes 262176 | tf_op jit(solution)/shard_map/ppermute | solution.py:16
  (84 shorter events, 10.5 us)
Async XLA Ops:
  0.0 264.3 %copy-start = (bf16[1,1024,32]{1,2,0:T(8,128)(2,1)S(1)}, bf16[1,1024,32]{1,2,0:T(8,128)(2,1)}, u32[]{:S(2)}) copy-start(bf16[1,1024,32]{1,2,0:T(8,128)(2,1)} %param.16) | copy-start | bytes 196612
  8.5 81.2 %copy-start.7 = (bf16[1,16,1024]{2,1,0:T(8,128)(2,1)S(1)}, bf16[1,16,1024]{2,1,0:T(8,128)(2,1)}, u32[]{:S(2)}) copy-start(bf16[1,16,1024]{2,1,0:T(8,128)(2,1)} %param.15) | copy-start | bytes 98308
  91.4 9.9 %copy-start.3 = (bf16[1,1024,512]{2,1,0:T(8,128)(2,1)S(1)}, bf16[1,1024,512]{2,1,0:T(8,128)(2,1)}, u32[]{:S(2)}) copy-start(bf16[1,1024,512]{2,1,0:T(8,128)(2,1)} %param.17) | copy-start | bytes 3145732
  91.4 61.2 %all-to-all-start.1 = ((bf16[64,1,16,1024]{3,2,1,0:T(8,128)(2,1)}), bf16[64,1,16,1024]{3,2,1,0:T(8,128)(2,1)S(1)}, u32[]{:S(2)}, u32[]{:S(2)}) async-start(bf16[64,1,16,1024]{3,2,1,0:T(8,128)(2,1)} %stack.2), calls=%async_computation.1 | async-start | bytes 4194304 | tf_op jit(solution)/shard_map/all_to_all | solution.py:131
  101.2 5.2 %copy-start.8 = (s32[1,128,2]{1,2,0:T(2,128)S(1)}, s32[1,128,2]{1,2,0:T(2,128)}, u32[]{:S(2)}) copy-start(s32[1,128,2]{1,2,0:T(2,128)} %param.14) | copy-start | bytes 3076
  101.2 5.6 %copy-start.10 = (s32[1,1,4]{2,1,0:T(1,128)S(1)}, s32[1,1,4]{2,1,0:T(1,128)}, u32[]{:S(2)}) copy-start(s32[1,1,4]{2,1,0:T(1,128)} %param.12) | copy-start | bytes 52
  101.3 5.8 %copy-start.11 = (s32[1,1,4]{2,1,0:T(1,128)S(1)}, s32[1,1,4]{2,1,0:T(1,128)}, u32[]{:S(2)}) copy-start(s32[1,1,4]{2,1,0:T(1,128)} %param.13) | copy-start | bytes 52
  101.3 6.8 %copy-start.9 = (s32[1,2,32]{2,1,0:T(2,128)S(1)}, s32[1,2,32]{2,1,0:T(2,128)}, u32[]{:S(2)}) copy-start(s32[1,2,32]{2,1,0:T(2,128)} %param.11) | copy-start | bytes 772
  104.1 134.6 %collective-permute-start = (bf16[1024,1024]{1,0:T(8,128)(2,1)}, bf16[1024,1024]{1,0:T(8,128)(2,1)}, u32[]{:S(2)}, u32[]{:S(2)}) collective-permute-start(bf16[1024,1024]{1,0:T(8,128)(2,1)} %pad_maximum_fusion.1), channel_id=1, source_target_pairs={{0,1},{1,0},{2,3},{3,2},{4,5},{5,4},{6,7},{7,6},{8,9},{9,8},{10,11... | collective-permute-start | bytes 6291464 | tf_op jit(solution)/shard_map/ppermute | solution.py:10
  157.1 7.9 %copy-start.2 = (bf16[1,512,1024]{2,1,0:T(8,128)(2,1)S(1)}, bf16[1,512,1024]{2,1,0:T(8,128)(2,1)}, u32[]{:S(2)}) copy-start(bf16[1,512,1024]{2,1,0:T(8,128)(2,1)} %param.19) | copy-start | bytes 3145732
  157.1 84.7 %all-to-all-start.2 = ((bf16[64,8,1024]{2,1,0:T(8,128)(2,1)}), bf16[64,8,1024]{2,1,0:T(8,128)(2,1)}, u32[]{:S(2)}, u32[]{:S(2)}) async-start(bf16[64,8,1024]{2,1,0:T(8,128)(2,1)} %bitcast.21), calls=%async_computation.2 | async-start | bytes 2097152 | tf_op jit(solution)/shard_map/all_to_all | solution.py:171
  165.0 69.6 %collective-permute-start.1 = (bf16[512,1024]{1,0:T(8,128)(2,1)S(1)}, bf16[512,1024]{1,0:T(8,128)(2,1)}, u32[]{:S(2)}, u32[]{:S(2)}) collective-permute-start(bf16[512,1024]{1,0:T(8,128)(2,1)S(1)} %bitcast.110), channel_id=1, source_target_pairs={{0,1},{1,0},{2,3},{3,2},{4,5},{5,4},{6,7},{7,6},{8,9},{9,8},{10,11... | collective-permute-start | bytes 3145736 | tf_op jit(solution)/shard_map/ppermute | solution.py:10
  238.7 3.1 %copy-start.4 = (bf16[1,1024,512]{2,1,0:T(8,128)(2,1)S(1)}, bf16[1,1024,512]{2,1,0:T(8,128)(2,1)}, u32[]{:S(2)}) copy-start(bf16[1,1024,512]{2,1,0:T(8,128)(2,1)} %param.17) | copy-start | bytes 3145732
  241.8 3.3 %copy-start.5 = (bf16[1,1024,512]{2,1,0:T(8,128)(2,1)S(1)}, bf16[1,1024,512]{2,1,0:T(8,128)(2,1)}, u32[]{:S(2)}) copy-start(bf16[1,1024,512]{2,1,0:T(8,128)(2,1)} %param.18) | copy-start | bytes 3145732
  241.8 3.3 %copy-start.6 = (bf16[1024,512]{1,0:T(8,128)(2,1)S(1)}, bf16[1024,512]{1,0:T(8,128)(2,1)}, u32[]{:S(2)}) copy-start(bf16[1024,512]{1,0:T(8,128)(2,1)} %get-tuple-element.11) | copy-start | bytes 3145732
  245.1 3.8 %copy-start.1 = (bf16[1024,1024]{1,0:T(8,128)(2,1)S(1)}, bf16[1024,1024]{1,0:T(8,128)(2,1)}, u32[]{:S(2)}) copy-start(bf16[1024,1024]{1,0:T(8,128)(2,1)} %maximum_select_fusion) | copy-start | bytes 6291460
  251.3 40.9 %all-to-all-start.3 = ((bf16[64,8,1024]{2,1,0:T(8,128)(2,1)}), bf16[64,8,1024]{2,1,0:T(8,128)(2,1)S(1)}, u32[]{:S(2)}, u32[]{:S(2)}) async-start(bf16[64,8,1024]{2,1,0:T(8,128)(2,1)} %fusion.16), calls=%async_computation.3 | async-start | bytes 2097152 | tf_op jit(solution)/shard_map/all_to_all | solution.py:173
  295.5 7.0 %collective-permute-start.2 = (bf16[1,128,1024]{2,1,0:T(8,128)(2,1)S(1)}, bf16[1,128,1024]{2,1,0:T(8,128)(2,1)S(1)}, u32[]{:S(2)}, u32[]{:S(2)}) collective-permute-start(bf16[1,128,1024]{2,1,0:T(8,128)(2,1)S(1)} %fusion.35), channel_id=1, source_target_pairs={{448,0},{0,64},{64,128},{128,192},{192,256},{256,320},{320,384},{3... | collective-permute-start | bytes 786440 | tf_op jit(solution)/shard_map/ppermute | solution.py:16
